TPU v7x, 32 devices: a whole 2x2x4 slice. The times are simulated.
32 devices in a mesh: member: 8 (over z, x), cell: 4 (over y, core).
Axes of the slice: x: 2, y: 2, z: 4, core: 2. Of those that a mesh axis runs over, the one named last changes fastest.
Arguments:
- latent: bfloat16 [8, 6144, 1024], P('member', 'cell'), may hold values from -6 to 6
- w_in: bfloat16 [1024, 1024], replicated, may hold values from -0.1875 to 0.1875
- w_out: bfloat16 [1024, 96], replicated, may hold values from -0.1875 to 0.1875
- target: bfloat16 [96, 6144], P(None, 'cell'), may hold values from -6 to 6
- cell_mask: int32 [6144], P('cell'), may hold values 0 or 1
Outputs:
- grad_w_in: float32 [1024, 1024], P(('member', 'cell'))
- grad_w_out: float32 [1024, 96], P(('member', 'cell'))
All inputs are finite; a program needn't handle non-finite values. No bound on the sum of `cell_mask` on one device may be relied on, other than what follows from the above.
Results may differ from a plain program's by a relative error of at most 0.0055.
Values may be sent and summed in bfloat16 or wider, within the bound.
A program may use at most 64 MiB of HBM per device.

v0:
```python
import jax
import jax.numpy as jnp
from jax import lax
from jax.sharding import PartitionSpec as P


def kernel_fn(diff):
    return diff / jnp.sqrt(1.0 + diff * diff)


def silu_slope(pre):
    gate = jax.nn.sigmoid(pre)
    return gate * (1.0 + pre * (1.0 - gate))


def per_device(latent, w_in, w_out, target, cell_mask):
    members = lax.axis_size("member")
    cell_count = lax.axis_size("cell")
    own_latent = latent[0]
    cells_here = own_latent.shape[0]
    scale = 1.0 / jnp.sqrt(jnp.float32(cells_here * cell_count))
    pre = jnp.dot(own_latent, w_in, preferred_element_type=jnp.float32)
    hidden = jax.nn.silu(pre).astype(jnp.bfloat16)
    fields = lax.dot_general(
        w_out, hidden, (((0,), (1,)), ((), ())), preferred_element_type=jnp.float32
    ).astype(jnp.bfloat16)
    wide = fields.astype(jnp.float32)
    pair = jnp.sum(
        kernel_fn(
            wide[None]
            - lax.all_gather(fields[None], "member", axis=0, tiled=True).astype(jnp.float32)
        ),
        axis=0,
    )
    weight = cell_mask.astype(jnp.float32) * scale / members
    own_term = kernel_fn(wide - target.astype(jnp.float32))
    grad_fields = (weight[None] * (own_term - pair / members)).astype(jnp.bfloat16)
    back = lax.dot_general(
        grad_fields, w_out, (((0,), (1,)), ((), ())), preferred_element_type=jnp.float32
    )
    grad_pre = (back * silu_slope(pre)).astype(jnp.bfloat16)
    width = w_in.shape[1]
    grad_in = lax.dot_general(
        own_latent, grad_pre, (((0,), (0,)), ((), ())), preferred_element_type=jnp.float32
    )
    grad_out = lax.dot_general(
        hidden, grad_fields, (((0,), (1,)), ((), ())), preferred_element_type=jnp.float32
    )
    owned = lax.psum_scatter(
        jnp.concatenate([grad_in, grad_out], axis=1),
        ("member", "cell"),
        scatter_dimension=0,
        tiled=True,
    )
    return (owned[:, :width], owned[:, width:])


def solution(mesh):
    in_specs = (P("member", "cell", None), P(), P(), P(None, "cell"), P("cell"))
    out_specs = (P(("member", "cell"), None), P(("member", "cell"), None))
    return jax.shard_map(
        per_device, mesh=mesh, in_specs=in_specs, out_specs=out_specs, check_vma=False
    )
```

profile of v0, /device:TPU:0, one launch (start us, length us, event | category | flops | bytes accessed | tf_op | source)
XLA Modules:
  0.0 217.5 jit_solution(14600535981441059085)
XLA Ops:
  7.2 0.0 copy-start
  7.2 0.0 all-gather.3.cloned.1.call-start
  7.2 1.8 copy-done
  9.1 0.0 copy-start.5
  9.1 7.5 %multiply_convert_fusion.1 = (bf16[1536,1024]{1,0:T(8,128)(2,1)S(1)}, f32[1536,1024]{1,0:T(8,128)}) fusion(bf16[1024,1024]{1,0:T(8,128)(2,1)} %param.6, bf16[1,1536,1024]{2,1,0:T(8,128)(2,1)S(1)} %copy-done), kind=kOutput, calls=%fused_computation.1 | convolution fusion | flops 3229089792 | bytes 14680064 | tf_op jit(solution)/shard_map/dot_general | solution.py:22
  16.6 0.0 copy-start.1
  16.6 0.0 copy-start.6
  16.6 1.7 copy-done.1
  18.3 0.0 copy-done.5
  18.3 0.0 copy-start.4
  18.3 2.0 fusion.14
  20.3 0.0 all-gather.3.cloned.1.call-update
  20.4 0.0 reduce-scatter.4.cloned.1.call-start
  20.4 0.0 copy-done.6
  20.4 54.6 %all-gather.3.cloned.1.call-done = bf16[768,1536]{1,0:T(8,128)(2,1)} async-done(((bf16[96,1536]{1,0:T(8,128)(2,1)}), bf16[768,1536]{1,0:T(8,128)(2,1)}) %all-gather.3.cloned.1.call-update) | async-done | bytes 2359312 | tf_op jit(solution)/shard_map/all_gather | solution.py:31
  75.0 0.0 copy-start.2
  75.1 3.1 %fusion.4 = f32[96,1536]{1,0:T(8,128)S(1)} fusion(bf16[8,96,1536]{2,1,0:T(8,128)(2,1)} %bitcast.23, f32[96,1536]{1,0:T(8,128)} %get-tuple-element.8), kind=kLoop, calls=%fused_computation.8 | loop fusion | flops 6930432 | bytes 3538944 | tf_op jit(solution)/shard_map/reduce_sum | solution.py:28
  78.1 0.0 copy-done.4
  78.1 1.2 multiply_convert_fusion.2
  79.3 0.0 copy-done.2
  79.3 0.0 copy-start.3
  79.3 0.6 fusion.15
  80.0 0.1 copy-done.3
  80.0 10.6 %fusion.10 = f32[1024,1024]{0,1:T(8,128)} fusion(bf16[1,1536,1024]{2,1,0:T(8,128)(2,1)S(1)} %copy-done, f32[1536,1024]{1,0:T(8,128)} %get-tuple-element.7, bf16[96,1536]{1,0:T(8,128)(2,1)} %copy-done.3, bf16[1024,96]{0,1:T(8,128)(2,1)} %param.7), kind=kOutput, calls=%fused_computation.16 | convolution fusion | flops 3537371136 | bytes 14123008 | tf_op jit(solution)/shard_map/dot_general | solution.py:43
  90.7 5.0 %pad_maximum_fusion = f32[1024,1120]{0,1:T(8,128)} fusion(f32[1024,96]{0,1:T(8,128)S(1)} %fusion.15, f32[1024,1024]{0,1:T(8,128)} %fusion.10), kind=kLoop, calls=%fused_computation.9 | loop fusion | flops 1146880 | bytes 9175040 | tf_op jit(solution)/shard_map/concatenate | solution.py:50
  95.7 5.9 %copy.11 = f32[1024,1120]{1,0:T(8,128)} copy(f32[1024,1120]{0,1:T(8,128)} %pad_maximum_fusion) | data formatting | bytes 9175040
  101.6 0.0 reduce-scatter.4.cloned.1.call-update
  101.6 106.2 %reduce-scatter.4.cloned.1.call-done = f32[32,1120]{1,0:T(8,128)} async-done(((f32[1024,1120]{1,0:T(8,128)}), f32[32,1120]{1,0:T(8,128)}) %reduce-scatter.4.cloned.1.call-update) | async-done | bytes 143376
  207.8 1.6 slice.8
  209.3 1.3 slice.9
  (1 shorter events, 0.0 us)
Async XLA Ops:
  7.2 1.9 copy-start
  7.2 67.9 %all-gather.3.cloned.1.call-start = ((), (), s32[]{:S(2)}) async-start(), calls=%async_computation.1 | async-start | bytes 2654208 | tf_op jit(solution)/shard_map/all_gather | solution.py:31
  9.1 9.2 %copy-start.5 = (bf16[1024,96]{0,1:T(8,128)(2,1)S(1)}, bf16[1024,96]{0,1:T(8,128)(2,1)}, u32[]{:S(2)}) copy-start(bf16[1024,96]{0,1:T(8,128)(2,1)} %param.7) | copy-start | bytes 589828
  16.6 1.7 copy-start.1
  16.6 3.8 %copy-start.6 = (s32[1536]{0:T(1024)S(1)}, s32[1536]{0:T(1024)}, u32[]{:S(2)}) copy-start(s32[1536]{0:T(1024)} %param.9) | copy-start | bytes 18436
  18.3 59.8 %copy-start.4 = (bf16[96,1536]{1,0:T(8,128)(2,1)S(1)}, bf16[96,1536]{1,0:T(8,128)(2,1)}, u32[]{:S(2)}) copy-start(bf16[96,1536]{1,0:T(8,128)(2,1)} %param.8) | copy-start | bytes 884740
  20.4 187.4 %reduce-scatter.4.cloned.1.call-start = ((), (), s32[]{:S(2)}) async-start(), calls=%async_computation.2 | async-start | bytes 4866048
  75.0 4.3 %copy-start.2 = (bf16[1536,1024]{1,0:T(8,128)(2,1)S(1)}, bf16[1536,1024]{1,0:T(8,128)(2,1)}, u32[]{:S(2)}) copy-start(bf16[1536,1024]{1,0:T(8,128)(2,1)} %copy-done.1) | copy-start | bytes 9437188
  79.3 0.7 copy-start.3
Sparse Core Ops, SparseCore 0:
  20.5 54.5 all-gather.2
  101.7 105.9 reduce-scatter.3
where the time goes:
time: 218 us
  waiting for transfers between devices  161 us (74%)
  matrix products  20.8 us (10%)
  between operations  14.1 us (6%)
  local copies, waits for them, and re-layouts  12.5 us (6%)
  other arithmetic  9.23 us (4%)
    unnamed x3, waiting for transfers between devices  106 us
    all_gather x1, waiting for transfers between devices, per_device(): lax.all_gather(fields[None], 'member', axis=0, tiled=True)  54.6 us
    dot_general x1, matrix products, per_device(): lax.dot_general(own_latent, grad_pre, (((0,), (0,)), ((), ())), preferred...  10.6 us
    unnamed x15, local copies, waits for them, and re-layouts  9.56 us
    dot_general x1, matrix products, per_device(): pre = jnp.dot(own_latent, w_in, preferred_element_type=jnp.float32)  7.54 us
    concatenate x1, other arithmetic, per_device(): jnp.concatenate([grad_in, grad_out], axis=1)  4.99 us
  transfers between devices with their start and end apart: 2, of which 2 were waited for; matrix products, arithmetic and copies ran while one was open for 0% of the time, Pallas kernels for 0%

commit v1 on v0

--- a/solution.py
+++ b/solution.py
@@ -2,6 +2,18 @@
 import jax.numpy as jnp
 from jax import lax
 from jax.sharding import PartitionSpec as P
+
+
+def direct_sectors(array_here, shard_axis):
+    return jnp.concatenate(
+        lax.all_to_all(
+            jnp.stack([array_here] * lax.axis_size(shard_axis)),
+            shard_axis,
+            split_axis=0,
+            concat_axis=0,
+        ),
+        axis=0,
+    )
 
 
 def kernel_fn(diff):
@@ -26,11 +38,7 @@
     ).astype(jnp.bfloat16)
     wide = fields.astype(jnp.float32)
     pair = jnp.sum(
-        kernel_fn(
-            wide[None]
-            - lax.all_gather(fields[None], "member", axis=0, tiled=True).astype(jnp.float32)
-        ),
-        axis=0,
+        kernel_fn(wide[None] - direct_sectors(fields[None], "member").astype(jnp.float32)), axis=0
     )
     weight = cell_mask.astype(jnp.float32) * scale / members
     own_term = kernel_fn(wide - target.astype(jnp.float32))

time: 218 us -> 227 us (1.041)
  starting transfers between devices: 0.08 us -> 7.32 us
    all_gather x1 -> x0, waiting for transfers between devices: 54.6 us -> none  [per_device(): lax.all_gather(fields[None], 'member', axis=0, tiled=True)]
    all_to_all x0 -> x1, waiting for transfers between devices: none -> 53.9 us  [direct_sectors(): lax.all_to_all(jnp.stack([array_here] * lax.axis_size(shard_axis)), shard...]
    all_to_all x0 -> x1, starting transfers between devices: none -> 7.28 us  [direct_sectors(): lax.all_to_all(jnp.stack([array_here] * lax.axis_size(shard_axis)), shard...]
    unnamed x3 -> x2, waiting for transfers between devices: 106 us -> 107 us
    unnamed x15 -> x13, local copies, waits for them, and re-layouts: 9.56 us -> 9.61 us
where the time goes in v1:
time: 227 us; the launch traced here: 226 us
  waiting for transfers between devices  161 us (71%)
  matrix products  20.7 us (9%)
  local copies, waits for them, and re-layouts  14.2 us (6%)
  between operations  14.1 us (6%)
  other arithmetic  9.24 us (4%)
  starting transfers between devices  7.32 us (3%)
    unnamed x2, waiting for transfers between devices  107 us
    all_to_all x1, waiting for transfers between devices, direct_sectors(): lax.all_to_all(jnp.stack([array_here] * lax.axis_size(shard_axis)), shard...  53.9 us
    dot_general x1, matrix products, per_device(): lax.dot_general(own_latent, grad_pre, (((0,), (0,)), ((), ())), preferred...  10.7 us
    unnamed x13, local copies, waits for them, and re-layouts  9.61 us
    dot_general x1, matrix products, per_device(): pre = jnp.dot(own_latent, w_in, preferred_element_type=jnp.float32)  7.49 us
    all_to_all x1, starting transfers between devices, direct_sectors(): lax.all_to_all(jnp.stack([array_here] * lax.axis_size(shard_axis)), shard...  7.28 us
    concatenate x1, other arithmetic, per_device(): jnp.concatenate([grad_in, grad_out], axis=1)  5 us
  transfers between devices with their start and end apart: 2, of which 2 were waited for; matrix products, arithmetic and copies ran while one was open for 0% of the time, Pallas kernels for 0%

profile of v1, /device:TPU:0, one launch (start us, length us, event | category | flops | bytes accessed | tf_op | source)
XLA Modules:
  0.0 226.4 jit_solution(4223334116127603561)
XLA Ops:
  7.2 0.0 copy-start
  7.2 0.0 copy-start.4
  7.2 1.9 copy-done
  9.1 7.5 %multiply_convert_fusion.1 = (bf16[1536,1024]{1,0:T(8,128)(2,1)S(1)}, f32[1536,1024]{1,0:T(8,128)}) fusion(bf16[1024,1024]{1,0:T(8,128)(2,1)} %param.6, bf16[1,1536,1024]{2,1,0:T(8,128)(2,1)S(1)} %copy-done), kind=kOutput, calls=%fused_computation.1 | convolution fusion | flops 3229089792 | bytes 14680064 | tf_op jit(solution)/shard_map/dot_general | solution.py:34
  16.5 0.0 copy-start.1
  16.5 1.7 copy-done.1
  18.2 0.0 copy-done.4
  18.2 1.9 fusion.14
  20.2 0.0 copy-start.5
  20.2 1.7 stack.3
  21.8 7.3 %all-to-all-start = ((bf16[8,1,96,1536]{3,2,1,0:T(8,128)(2,1)}), bf16[8,1,96,1536]{3,2,1,0:T(8,128)(2,1)}, u32[]{:S(2)}, u32[]{:S(2)}) async-start(bf16[8,1,96,1536]{3,2,1,0:T(8,128)(2,1)} %stack.3), calls=%async_computation | async-start | bytes 4718592 | tf_op jit(solution)/shard_map/all_to_all | solution.py:9
  29.1 0.0 reduce-scatter.4.cloned.1.call-start
  29.2 0.0 copy-done.5
  29.2 53.9 %all-to-all-done = bf16[8,1,96,1536]{3,2,1,0:T(8,128)(2,1)} async-done(((bf16[8,1,96,1536]{3,2,1,0:T(8,128)(2,1)}), bf16[8,1,96,1536]{3,2,1,0:T(8,128)(2,1)}, u32[]{:S(2)}, u32[]{:S(2)}) %all-to-all-start) | async-done | bytes 2359328 | tf_op jit(solution)/shard_map/all_to_all | solution.py:9
  83.1 0.0 copy-start.2
  83.1 3.1 %fusion.4 = f32[96,1536]{1,0:T(8,128)S(1)} fusion(bf16[8,1,96,1536]{3,2,1,0:T(8,128)(2,1)} %all-to-all-done, f32[96,1536]{1,0:T(8,128)} %get-tuple-element.8), kind=kLoop, calls=%fused_computation.8 | loop fusion | flops 6930432 | bytes 3538944 | tf_op jit(solution)/shard_map/reduce_sum | solution.py:40
  86.2 1.2 multiply_convert_fusion.2
  87.3 0.0 copy-done.2
  87.3 0.0 copy-start.3
  87.4 0.6 fusion.15
  88.0 0.1 copy-done.3
  88.1 10.7 %fusion.10 = f32[1024,1024]{0,1:T(8,128)} fusion(bf16[1,1536,1024]{2,1,0:T(8,128)(2,1)S(1)} %copy-done, f32[1536,1024]{1,0:T(8,128)} %get-tuple-element.7, bf16[96,1536]{1,0:T(8,128)(2,1)} %copy-done.3, bf16[1024,96]{0,1:T(8,128)(2,1)} %param.7), kind=kOutput, calls=%fused_computation.16 | convolution fusion | flops 3537371136 | bytes 14123008 | tf_op jit(solution)/shard_map/dot_general | solution.py:51
  98.7 5.0 %pad_maximum_fusion = f32[1024,1120]{0,1:T(8,128)} fusion(f32[1024,96]{0,1:T(8,128)S(1)} %fusion.15, f32[1024,1024]{0,1:T(8,128)} %fusion.10), kind=kLoop, calls=%fused_computation.9 | loop fusion | flops 1146880 | bytes 9175040 | tf_op jit(solution)/shard_map/concatenate | solution.py:58
  103.7 6.0 %copy.11 = f32[1024,1120]{1,0:T(8,128)} copy(f32[1024,1120]{0,1:T(8,128)} %pad_maximum_fusion) | data formatting | bytes 9175040
  109.7 0.0 reduce-scatter.4.cloned.1.call-update
  109.7 106.9 %reduce-scatter.4.cloned.1.call-done = f32[32,1120]{1,0:T(8,128)} async-done(((f32[1024,1120]{1,0:T(8,128)}), f32[32,1120]{1,0:T(8,128)}) %reduce-scatter.4.cloned.1.call-update) | async-done | bytes 143376
  216.6 1.6 slice.8
  218.2 1.3 slice.9
  (1 shorter events, 0.0 us)
Async XLA Ops:
  7.2 1.9 copy-start
  7.2 11.1 %copy-start.4 = (bf16[1024,96]{0,1:T(8,128)(2,1)S(1)}, bf16[1024,96]{0,1:T(8,128)(2,1)}, u32[]{:S(2)}) copy-start(bf16[1024,96]{0,1:T(8,128)(2,1)} %param.7) | copy-start | bytes 589828
  16.5 1.7 copy-start.1
  20.2 9.0 %copy-start.5 = (s32[1536]{0:T(1024)S(1)}, s32[1536]{0:T(1024)}, u32[]{:S(2)}) copy-start(s32[1536]{0:T(1024)} %param.9) | copy-start | bytes 18436
  21.8 61.2 %all-to-all-start = ((bf16[8,1,96,1536]{3,2,1,0:T(8,128)(2,1)}), bf16[8,1,96,1536]{3,2,1,0:T(8,128)(2,1)}, u32[]{:S(2)}, u32[]{:S(2)}) async-start(bf16[8,1,96,1536]{3,2,1,0:T(8,128)(2,1)} %stack.3), calls=%async_computation | async-start | bytes 4718592 | tf_op jit(solution)/shard_map/all_to_all | solution.py:9
  29.1 187.5 %reduce-scatter.4.cloned.1.call-start = ((), (), s32[]{:S(2)}) async-start(), calls=%async_computation.2 | async-start | bytes 4866048
  83.1 4.2 %copy-start.2 = (bf16[1536,1024]{1,0:T(8,128)(2,1)S(1)}, bf16[1536,1024]{1,0:T(8,128)(2,1)}, u32[]{:S(2)}) copy-start(bf16[1536,1024]{1,0:T(8,128)(2,1)} %copy-done.1) | copy-start | bytes 9437188
  87.3 0.7 copy-start.3
Sparse Core Ops, SparseCore 0:
  109.8 106.7 reduce-scatter.3
